TPU v7x, 256 devices: a whole 4x4x8 slice. The times are simulated.
256 devices in a mesh: lat: 8 (over x, core), lon: 32 (over z, y).
Axes of the slice: x: 4, y: 4, z: 8, core: 2. Of those that a mesh axis runs over, the one named last changes fastest.
Arguments:
- features: bfloat16 [256, 512, 768], P('lat', 'lon'), may hold values from -6 to 6
- cotangent: bfloat16 [256, 512, 768], P('lat', 'lon'), may hold values from -6 to 6
- weight_first: bfloat16 [2, 8, 96, 96], replicated, may hold values from -1 to 1
- weight_second: bfloat16 [2, 8, 96, 96], replicated, may hold values from -1 to 1
Outputs:
- mixed_field: bfloat16 [256, 512, 768], P('lat', 'lon')
- feature_grad: bfloat16 [256, 512, 768], P('lat', 'lon')
- grad_first: float32 [2, 8, 96, 96], replicated
- grad_second: float32 [2, 8, 96, 96], replicated
All inputs are finite; a program needn't handle non-finite values.
Results may differ from a plain program's by a relative error of at most 0.012.
The roundings to bfloat16 on the way count: a program that leaves them out, or rounds other values in their place, can miss the bound.
Values may be sent and summed in bfloat16 or wider, within the bound.
A program may use at most 64 MiB of HBM per device.

v0:
```python
import math
import jax
import jax.numpy as jnp
from jax import lax
from jax.sharding import PartitionSpec as P

NB = 8
BS = 96
KWD = 1
shrink_level = 0.01
gelu_coeff = 0.7978845608028654


def wave_table(first, second, length):
    product = first[:, None] * second[None, :] % length
    angle = 2.0 * math.pi / length * product.astype(jnp.float32)
    return (jnp.cos(angle) / math.sqrt(length), jnp.sin(angle) / math.sqrt(length))


def batch_product(left, weights):
    return jnp.einsum("mbi,bio->mbo", left, weights, preferred_element_type=jnp.float32)


def batch_back(left, weights):
    return jnp.einsum("mbo,bio->mbi", left, weights, preferred_element_type=jnp.float32)


def batch_outer(left, right):
    return jnp.einsum("mbi,mbo->bio", left, right, preferred_element_type=jnp.float32)


def gelu_parts(values):
    squared = values * values
    tangent = jnp.tanh(gelu_coeff * (values + 0.044715 * squared * values))
    result = 0.5 * values * (1.0 + tangent)
    slope = 0.5 * (1.0 + tangent) + 0.5 * values * (1.0 - tangent * tangent) * gelu_coeff * (
        1.0 + 3.0 * 0.044715 * squared
    )
    return (result, slope)


def shrink_parts(values):
    ratio = jnp.tanh(values / shrink_level)
    return (values - shrink_level * ratio, ratio * ratio)


def spectral_block(real_in, imag_in, real_cot, imag_cot, mode_weight, weight_first, weight_second):
    first_re, first_im = (weight_first[0], weight_first[1])
    second_re, second_im = (weight_second[0], weight_second[1])
    pre_real = batch_product(real_in, first_re) - batch_product(imag_in, first_im)
    pre_imag = batch_product(real_in, first_im) + batch_product(imag_in, first_re)
    act_real, slope_real = gelu_parts(pre_real)
    act_imag, slope_imag = gelu_parts(pre_imag)
    hidden_real = act_real.astype(jnp.bfloat16)
    hidden_imag = act_imag.astype(jnp.bfloat16)
    post_real = batch_product(hidden_real, second_re) - batch_product(hidden_imag, second_im)
    post_imag = batch_product(hidden_real, second_im) + batch_product(hidden_imag, second_re)
    shr_real, pass_real = shrink_parts(post_real)
    shr_imag, pass_imag = shrink_parts(post_imag)
    out_real = shr_real.astype(jnp.bfloat16)
    out_imag = shr_imag.astype(jnp.bfloat16)
    grad_post_real = (mode_weight * real_cot.astype(jnp.float32) * pass_real).astype(jnp.bfloat16)
    grad_post_imag = (mode_weight * imag_cot.astype(jnp.float32) * pass_imag).astype(jnp.bfloat16)
    grad_hid_real = batch_back(grad_post_real, second_re) + batch_back(grad_post_imag, second_im)
    grad_hid_imag = batch_back(grad_post_imag, second_re) - batch_back(grad_post_real, second_im)
    grad_pre_real = (grad_hid_real * slope_real).astype(jnp.bfloat16)
    grad_pre_imag = (grad_hid_imag * slope_imag).astype(jnp.bfloat16)
    back_real = (batch_back(grad_pre_real, first_re) + batch_back(grad_pre_imag, first_im)).astype(
        jnp.bfloat16
    )
    back_imag = (batch_back(grad_pre_imag, first_re) - batch_back(grad_pre_real, first_im)).astype(
        jnp.bfloat16
    )
    grad_second = jnp.stack(
        [
            batch_outer(hidden_real, grad_post_real) + batch_outer(hidden_imag, grad_post_imag),
            batch_outer(hidden_real, grad_post_imag) - batch_outer(hidden_imag, grad_post_real),
        ]
    )
    grad_first = jnp.stack(
        [
            batch_outer(real_in, grad_pre_real) + batch_outer(imag_in, grad_pre_imag),
            batch_outer(real_in, grad_pre_imag) - batch_outer(imag_in, grad_pre_real),
        ]
    )
    return (out_real, out_imag, back_real, back_imag, grad_first, grad_second)


def lon_transpose(source, split_dim, concat_dim):
    return lax.all_to_all(source, "lon", split_axis=split_dim, concat_axis=concat_dim, tiled=True)


def shards(features, cotangent, weight_first, weight_second):
    lat_count = lax.axis_size("lat")
    lon_count = lax.axis_size("lon")
    lat_index = lax.axis_index("lat")
    lon_index = lax.axis_index("lon")
    band_rows, band_cols, channels = features.shape
    rows_total = band_rows * lat_count
    cols_total = band_cols * lon_count
    rows_each = band_rows // lon_count
    kept_total = KWD * lat_count * lon_count
    stacked = jnp.stack([features, cotangent])
    full_rows = lon_transpose(stacked, 1, 2)
    lon_cos, lon_sin = wave_table(
        jnp.arange(kept_total, dtype=jnp.int32), jnp.arange(cols_total, dtype=jnp.int32), cols_total
    )
    lon_coeffs = jnp.concatenate([lon_cos, lon_sin]).astype(jnp.bfloat16)
    product = jnp.einsum(
        "aw,rwc->rac",
        lon_coeffs,
        full_rows.reshape(2 * rows_each, cols_total, channels),
        preferred_element_type=jnp.float32,
    )
    spectral_rows = jnp.stack([product[:, :kept_total], -product[:, kept_total:]], axis=1).astype(
        jnp.bfloat16
    )
    spectral_rows = spectral_rows.reshape(2, rows_each, 2, kept_total, channels)
    gathered = lax.all_to_all(
        lax.all_to_all(spectral_rows, "lat", split_axis=3, concat_axis=1, tiled=True),
        "lon",
        split_axis=3,
        concat_axis=1,
        tiled=True,
    )
    position = jnp.arange(rows_total, dtype=jnp.int32)
    row_of = (
        position // rows_each % lat_count * band_rows
        + position // (lat_count * rows_each) * rows_each
        + position % rows_each
    )
    lat_cos, lat_sin = wave_table(jnp.arange(rows_total, dtype=jnp.int32), row_of, rows_total)
    lat_coeffs = jnp.concatenate([lat_cos, lat_sin]).astype(jnp.bfloat16)
    product = jnp.einsum(
        "ah,shrc->sarc",
        lat_coeffs,
        gathered.reshape(2, rows_total, 2, KWD * channels),
        preferred_element_type=jnp.float32,
    )
    upper = product[:, :rows_total]
    lower = product[:, rows_total:]
    spec_real = (upper[:, :, 0] + lower[:, :, 1]).astype(jnp.bfloat16)
    spec_imag = (upper[:, :, 1] - lower[:, :, 0]).astype(jnp.bfloat16)
    modes = rows_total * KWD
    held_kw = (lat_index * lon_count + lon_index) * KWD + jnp.arange(KWD, dtype=jnp.int32)
    mode_weight = jnp.broadcast_to(
        jnp.where(held_kw == 0, 1.0, 2.0).astype(jnp.float32)[None, :], (rows_total, KWD)
    ).reshape(modes, 1, 1)
    results = spectral_block(
        spec_real[0].reshape(modes, NB, BS),
        spec_imag[0].reshape(modes, NB, BS),
        spec_real[1].reshape(modes, NB, BS),
        spec_imag[1].reshape(modes, NB, BS),
        mode_weight,
        weight_first,
        weight_second,
    )
    out_real, out_imag, back_real, back_imag, grad_first, grad_second = results
    spec_out = jnp.stack(
        [jnp.stack([out_real, out_imag]), jnp.stack([back_real, back_imag])]
    ).reshape(2, 2, rows_total, KWD * channels)
    nat_cos, nat_sin = wave_table(
        jnp.arange(rows_total, dtype=jnp.int32), jnp.arange(rows_total, dtype=jnp.int32), rows_total
    )
    nat_coeffs = jnp.concatenate([nat_cos, nat_sin]).astype(jnp.bfloat16)
    product = jnp.einsum("ak,sqkc->saqc", nat_coeffs, spec_out, preferred_element_type=jnp.float32)
    upper = product[:, :rows_total]
    lower = product[:, rows_total:]
    inverse_rows = jnp.stack(
        [upper[:, :, 0] - lower[:, :, 1], lower[:, :, 0] + upper[:, :, 1]], axis=2
    ).astype(jnp.bfloat16)
    inverse_rows = inverse_rows.reshape(2, rows_total, 2, KWD, channels)
    returned = lax.all_to_all(
        lax.all_to_all(inverse_rows, "lat", split_axis=1, concat_axis=3, tiled=True),
        "lon",
        split_axis=1,
        concat_axis=3,
        tiled=True,
    )
    slot_index = jnp.arange(kept_total, dtype=jnp.int32)
    kw_of = (
        slot_index // KWD % lat_count * lon_count + slot_index // (lat_count * KWD)
    ) * KWD + slot_index % KWD
    inv_cos, inv_sin = wave_table(kw_of, jnp.arange(cols_total, dtype=jnp.int32), cols_total)
    plain = jnp.concatenate([inv_cos, -inv_sin]).astype(jnp.bfloat16)
    doubled = jnp.where(kw_of == 0, 1.0, 2.0).astype(jnp.float32)
    scaled = (plain.astype(jnp.float32) * jnp.concatenate([doubled, doubled])[:, None]).astype(
        jnp.bfloat16
    )
    returned_flat = returned.reshape(2, rows_each, 2 * kept_total, channels)
    filtered = jnp.einsum(
        "aw,rac->rwc", scaled, returned_flat[0], preferred_element_type=jnp.float32
    ).astype(jnp.bfloat16)
    backward = jnp.einsum(
        "aw,rac->rwc", plain, returned_flat[1], preferred_element_type=jnp.float32
    ).astype(jnp.bfloat16)
    spatial = lon_transpose(jnp.stack([filtered, backward]), 2, 1)
    mixed_field = (features.astype(jnp.float32) + spatial[0].astype(jnp.float32)).astype(
        jnp.bfloat16
    )
    feature_grad = (cotangent.astype(jnp.float32) + spatial[1].astype(jnp.float32)).astype(
        jnp.bfloat16
    )
    summed = lax.psum((grad_first, grad_second), ("lat", "lon"))
    factor = 1.0 / math.sqrt(rows_total * kept_total)
    return (mixed_field, feature_grad, summed[0] * factor, summed[1] * factor)


def solution(mesh):
    in_specs = (P("lat", "lon", None), P("lat", "lon", None), P(), P())
    out_specs = (P("lat", "lon", None), P("lat", "lon", None), P(), P())
    return jax.shard_map(shards, mesh=mesh, in_specs=in_specs, out_specs=out_specs, check_vma=False)
```

profile of v0, /device:TPU:2, one launch (start us, length us, event | category | flops | bytes accessed | tf_op | source)
XLA Modules:
  0.0 520.0 jit_solution(9959263662346330774)
XLA Ops:
  7.2 2.7 pad_maximum_fusion
  9.9 11.5 %all-to-all-start = ((bf16[2,32,16,768]{3,2,0,1:T(8,128)(2,1)}), bf16[2,32,16,768]{3,2,0,1:T(8,128)(2,1)S(1)}, u32[]{:S(2)}, u32[]{:S(2)}) async-start(bf16[2,32,16,768]{3,2,0,1:T(8,128)(2,1)} %pad_maximum_fusion), calls=%async_computation | async-start | bytes 3145728 | tf_op jit(solution)/shard_map/all_to_all | solution.py:90
  21.3 2.2 multiply_convert_fusion.7
  23.6 36.9 %all-to-all-done = bf16[2,32,16,768]{3,2,0,1:T(8,128)(2,1)S(1)} async-done(((bf16[2,32,16,768]{3,2,0,1:T(8,128)(2,1)}), bf16[2,32,16,768]{3,2,0,1:T(8,128)(2,1)S(1)}, u32[]{:S(2)}, u32[]{:S(2)}) %all-to-all-start) | async-done | bytes 1572896 | tf_op jit(solution)/shard_map/all_to_all | solution.py:90
  60.6 1.0 convolution_bitcast_fusion.2
  61.7 0.2 fusion.40
  62.1 1.9 copy.79
  64.0 25.0 %all_to_all.84 = bf16[2,1,2,256,768]{4,0,2,1,3:T(2,128)(2,1)S(1)} all-to-all(bf16[2,1,2,256,768]{4,0,2,1,3:T(2,128)(2,1)S(1)} %copy.79), channel_id=1, replica_groups=mesh['lat'=8,'lon'=32] {'lat'}, dimensions={3} | all-to-all | bytes 3145728 | tf_op jit(solution)/shard_map/all_to_all | solution.py:120
  89.2 2.0 copy.81
  91.2 5.9 %all-to-all-start.2 = ((bf16[2,8,2,32,768]{4,1,2,0,3:T(8,128)(2,1)}), bf16[2,8,2,32,768]{4,1,2,0,3:T(8,128)(2,1)S(1)}, u32[]{:S(2)}, u32[]{:S(2)}) async-start(bf16[2,8,2,32,768]{4,1,2,0,3:T(8,128)(2,1)} %copy.81), calls=%async_computation.2 | async-start | bytes 3145728 | tf_op jit(solution)/shard_map/all_to_all | solution.py:119
  97.2 1.1 multiply_convert_fusion.9
  98.3 1.1 multiply_convert_fusion.12
  99.5 36.3 %all-to-all-done.2 = bf16[2,8,2,32,768]{4,1,2,0,3:T(8,128)(2,1)S(1)} async-done(((bf16[2,8,2,32,768]{4,1,2,0,3:T(8,128)(2,1)}), bf16[2,8,2,32,768]{4,1,2,0,3:T(8,128)(2,1)S(1)}, u32[]{:S(2)}, u32[]{:S(2)}) %all-to-all-start.2) | async-done | bytes 1572896 | tf_op jit(solution)/shard_map/all_to_all | solution.py:119
  135.7 1.0 convolution_bitcast_fusion.1
  136.8 0.4 fusion.4
  137.2 0.6 copy-done.2
  137.8 0.3 fusion.88
  138.1 0.3 fusion.96
  138.5 0.5 multiply_convert_fusion.4
  138.9 0.5 copy-done.7
  139.4 0.3 fusion.84
  139.7 0.3 fusion.76
  140.2 0.5 multiply_convert_fusion.3
  140.7 0.4 subtract_convert_fusion.1
  141.1 0.2 fusion.79
  141.4 0.4 subtract_convert_fusion
  141.8 0.2 fusion.81
  142.1 0.6 fusion.27
  142.7 0.2 fusion.91
  142.9 0.6 fusion.28
  143.5 0.3 fusion.93
  143.8 0.3 fusion.29
  144.1 0.3 fusion.30
  144.3 1.0 convolution_bitcast_fusion
  145.3 0.2 fusion.41
  145.9 3.1 copy.98
  149.0 25.3 %all_to_all.85 = bf16[2,256,2,1,768]{4,0,3,2,1:T(2,128)(2,1)S(1)} all-to-all(bf16[2,256,2,1,768]{4,0,3,2,1:T(2,128)(2,1)} %copy.98), channel_id=1, replica_groups=mesh['lat'=8,'lon'=32] {'lat'}, dimensions={1} | all-to-all | bytes 3145728 | tf_op jit(solution)/shard_map/all_to_all | solution.py:174
  174.5 2.0 copy.100
  176.6 6.0 %all-to-all-start.4 = ((bf16[2,32,2,8,768]{4,3,2,0,1:T(8,128)(2,1)}), bf16[2,32,2,8,768]{4,3,2,0,1:T(8,128)(2,1)S(1)}, u32[]{:S(2)}, u32[]{:S(2)}) async-start(bf16[2,32,2,8,768]{4,3,2,0,1:T(8,128)(2,1)} %copy.100), calls=%async_computation.4 | async-start | bytes 3145728 | tf_op jit(solution)/shard_map/all_to_all | solution.py:173
  182.6 3.2 multiply_convert_fusion.6
  185.8 35.3 %all-to-all-done.4 = bf16[2,32,2,8,768]{4,3,2,0,1:T(8,128)(2,1)S(1)} async-done(((bf16[2,32,2,8,768]{4,3,2,0,1:T(8,128)(2,1)}), bf16[2,32,2,8,768]{4,3,2,0,1:T(8,128)(2,1)S(1)}, u32[]{:S(2)}, u32[]{:S(2)}) %all-to-all-start.4) | async-done | bytes 1572896 | tf_op jit(solution)/shard_map/all_to_all | solution.py:173
  221.3 0.8 copy-done.11
  222.2 0.6 fusion.18
  222.8 0.7 fusion.17
  223.7 3.0 copy.102
  226.6 5.8 %all-to-all-start.5 = ((bf16[2,1,512,768]{3,0,1,2:T(2,128)(2,1)}), bf16[2,1,512,768]{3,0,1,2:T(2,128)(2,1)S(1)}, u32[]{:S(2)}, u32[]{:S(2)}) async-start(bf16[2,1,512,768]{3,0,1,2:T(2,128)(2,1)} %copy.102), calls=%async_computation.5 | async-start | bytes 3145728 | tf_op jit(solution)/shard_map/all_to_all | solution.py:90
  232.5 1.3 fusion.127
  233.8 1.3 fusion.32
  235.1 0.3 fusion.128
  235.4 0.3 fusion.31
  235.7 0.9 pad_maximum_fusion.5
  236.6 0.2 fusion.125
  236.9 0.3 fusion.34
  237.1 0.2 fusion.126
  237.4 0.3 fusion.33
  237.7 0.9 pad_maximum_fusion.4
  238.6 264.8 %all-reduce.3.cloned.1.call-done = (f32[2,8,96,96]{3,2,1,0:T(8,128)}, f32[2,8,96,96]{3,2,1,0:T(8,128)}) async-done(((f32[2,8,96,96]{3,2,1,0:T(8,128)}, f32[2,8,96,96]{3,2,1,0:T(8,128)}), (f32[2,8,96,96]{3,2,1,0:T(8,128)}, f32[2,8,96,96]{3,2,1,0:T(8,128)})) %all-reduce.3.cloned.1.call-update) | async-done | bytes 1179664 | tf_op jit(solution)/shard_map/psum | solution.py:204
  503.4 2.2 broadcast_multiply_fusion
  505.6 0.9 broadcast_multiply_fusion.1
  506.5 2.2 fusion.123
  508.9 1.0 copy-done.8
  509.9 1.1 fusion.13
  511.1 1.0 copy-done.9
  512.1 1.1 fusion.14
  (43 shorter events, 2.0 us)
Async XLA Ops:
  9.9 50.6 %all-to-all-start = ((bf16[2,32,16,768]{3,2,0,1:T(8,128)(2,1)}), bf16[2,32,16,768]{3,2,0,1:T(8,128)(2,1)S(1)}, u32[]{:S(2)}, u32[]{:S(2)}) async-start(bf16[2,32,16,768]{3,2,0,1:T(8,128)(2,1)} %pad_maximum_fusion), calls=%async_computation | async-start | bytes 3145728 | tf_op jit(solution)/shard_map/all_to_all | solution.py:90
  91.2 44.5 %all-to-all-start.2 = ((bf16[2,8,2,32,768]{4,1,2,0,3:T(8,128)(2,1)}), bf16[2,8,2,32,768]{4,1,2,0,3:T(8,128)(2,1)S(1)}, u32[]{:S(2)}, u32[]{:S(2)}) async-start(bf16[2,8,2,32,768]{4,1,2,0,3:T(8,128)(2,1)} %copy.81), calls=%async_computation.2 | async-start | bytes 3145728 | tf_op jit(solution)/shard_map/all_to_all | solution.py:119
  136.8 1.0 copy-start.2
  138.4 1.0 copy-start.7
  141.1 1.8 copy-start.3
  141.8 0.9 copy-start.5
  143.5 0.8 copy-start
  176.6 44.5 %all-to-all-start.4 = ((bf16[2,32,2,8,768]{4,3,2,0,1:T(8,128)(2,1)}), bf16[2,32,2,8,768]{4,3,2,0,1:T(8,128)(2,1)S(1)}, u32[]{:S(2)}, u32[]{:S(2)}) async-start(bf16[2,32,2,8,768]{4,3,2,0,1:T(8,128)(2,1)} %copy.100), calls=%async_computation.4 | async-start | bytes 3145728 | tf_op jit(solution)/shard_map/all_to_all | solution.py:173
  221.2 1.0 copy-start.11
  221.2 1.0 copy-start.12
  226.6 279.9 %all-to-all-start.5 = ((bf16[2,1,512,768]{3,0,1,2:T(2,128)(2,1)}), bf16[2,1,512,768]{3,0,1,2:T(2,128)(2,1)S(1)}, u32[]{:S(2)}, u32[]{:S(2)}) async-start(bf16[2,1,512,768]{3,0,1,2:T(2,128)(2,1)} %copy.102), calls=%async_computation.5 | async-start | bytes 3145728 | tf_op jit(solution)/shard_map/all_to_all | solution.py:90
  232.4 271.0 %all-reduce.3.cloned.1.call-start = ((), (), s32[]{:S(2)}) async-start(), calls=%async_computation.6 | async-start | bytes 3145728 | tf_op jit(solution)/shard_map/psum | solution.py:204
  232.5 2.6 copy-start.6
  233.8 1.6 copy-start.4
  235.7 1.2 copy-start.1
  503.4 2.2 copy-start.10
  508.8 1.1 copy-start.8
  511.0 1.1 copy-start.9
Sparse Core Ops, SparseCore 0:
  239.4 263.9 all-reduce.2
where the time goes:
time: 521 us; the launch traced here: 520 us
  waiting for transfers between devices  373 us (72%)
  blocking collectives  50.3 us (10%)
  starting transfers between devices  29.2 us (6%)
  local copies, waits for them, and re-layouts  19.4 us (4%)
  other arithmetic  19 us (4%)
  between operations  14.6 us (3%)
  matrix products  14.2 us (3%)
    psum x1, waiting for transfers between devices, shards(): summed = lax.psum((grad_first, grad_second), ('lat', 'lon'))  265 us
    all_to_all x2, waiting for transfers between devices, lon_transpose(): lax.all_to_all(source, 'lon', split_axis=split_dim, concat_axis=concat_di...  36.9 us
    all_to_all x1, waiting for transfers between devices, shards(): lax.all_to_all(lax.all_to_all(spectral_rows, 'lat', split_axis=3, concat_...  36.3 us
    all_to_all x1, waiting for transfers between devices, shards(): lax.all_to_all(lax.all_to_all(inverse_rows, 'lat', split_axis=1, concat_a...  35.3 us
    all_to_all x1, blocking collectives, shards(): lax.all_to_all(inverse_rows, 'lat', split_axis=1, concat_axis=3, tiled=True)  25.3 us
    all_to_all x1, blocking collectives, shards(): lax.all_to_all(spectral_rows, 'lat', split_axis=3, concat_axis=1, tiled=T...  25 us
    all_to_all x2, starting transfers between devices, lon_transpose(): lax.all_to_all(source, 'lon', split_axis=split_dim, concat_axis=concat_di...  17.3 us
  transfers between devices with their start and end apart: 5, of which 4 were waited for; matrix products, arithmetic and copies ran while one was open for 3% of the time, Pallas kernels for 0%

commit v1 on v0

--- a/solution.py
+++ b/solution.py
@@ -3,6 +3,7 @@
 import jax.numpy as jnp
 from jax import lax
 from jax.sharding import PartitionSpec as P
+from jax.lax import psum
 
 NB = 8
 BS = 96
@@ -201,7 +202,7 @@
     feature_grad = (cotangent.astype(jnp.float32) + spatial[1].astype(jnp.float32)).astype(
         jnp.bfloat16
     )
-    summed = lax.psum((grad_first, grad_second), ("lat", "lon"))
+    summed = psum(psum((grad_first, grad_second), "lat"), "lon")
     factor = 1.0 / math.sqrt(rows_total * kept_total)
     return (mixed_field, feature_grad, summed[0] * factor, summed[1] * factor)
 

time: 521 us -> 479 us (0.919)
  waiting for transfers between devices: 373 us -> 329 us
    psum x1 -> x2, waiting for transfers between devices: 265 us -> 225 us  [shards(): summed = psum(psum((grad_first, grad_second), 'lat'), 'lon')]
  transfers between devices with their start and end apart: 5 -> 6, of which waited for: 4 -> 5; matrix products, arithmetic and copies ran while one was open for 3% -> 4% of each run, Pallas kernels for 0% -> 0%
where the time goes in v1:
time: 479 us; the launch traced here: 478 us
  waiting for transfers between devices  329 us (69%)
  blocking collectives  50.3 us (11%)
  starting transfers between devices  29.4 us (6%)
  other arithmetic  20.1 us (4%)
  local copies, waits for them, and re-layouts  19.5 us (4%)
  matrix products  15.4 us (3%)
  between operations  14.6 us (3%)
    psum x2, waiting for transfers between devices, shards(): summed = psum(psum((grad_first, grad_second), 'lat'), 'lon')  225 us
    all_to_all x2, waiting for transfers between devices, lon_transpose(): lax.all_to_all(source, 'lon', split_axis=split_dim, concat_axis=concat_di...  36.9 us
    all_to_all x1, waiting for transfers between devices, shards(): lax.all_to_all(lax.all_to_all(spectral_rows, 'lat', split_axis=3, concat_...  36.3 us
    all_to_all x1, waiting for transfers between devices, shards(): lax.all_to_all(lax.all_to_all(inverse_rows, 'lat', split_axis=1, concat_a...  30.7 us
    all_to_all x1, blocking collectives, shards(): lax.all_to_all(inverse_rows, 'lat', split_axis=1, concat_axis=3, tiled=True)  25.3 us
    all_to_all x1, blocking collectives, shards(): lax.all_to_all(spectral_rows, 'lat', split_axis=3, concat_axis=1, tiled=T...  25 us
    all_to_all x2, starting transfers between devices, lon_transpose(): lax.all_to_all(source, 'lon', split_axis=split_dim, concat_axis=concat_di...  17.4 us
  transfers between devices with their start and end apart: 6, of which 5 were waited for; matrix products, arithmetic and copies ran while one was open for 4% of the time, Pallas kernels for 0%

profile of v1, /device:TPU:2, one launch (start us, length us, event | category | flops | bytes accessed | tf_op | source)
XLA Modules:
  0.0 477.8 jit_solution(3756489223663425037)
XLA Ops:
  7.2 2.7 pad_maximum_fusion
  9.9 11.5 %all-to-all-start = ((bf16[2,32,16,768]{3,2,0,1:T(8,128)(2,1)}), bf16[2,32,16,768]{3,2,0,1:T(8,128)(2,1)S(1)}, u32[]{:S(2)}, u32[]{:S(2)}) async-start(bf16[2,32,16,768]{3,2,0,1:T(8,128)(2,1)} %pad_maximum_fusion), calls=%async_computation | async-start | bytes 3145728 | tf_op jit(solution)/shard_map/all_to_all | solution.py:91
  21.4 2.2 multiply_convert_fusion.7
  23.6 36.9 %all-to-all-done = bf16[2,32,16,768]{3,2,0,1:T(8,128)(2,1)S(1)} async-done(((bf16[2,32,16,768]{3,2,0,1:T(8,128)(2,1)}), bf16[2,32,16,768]{3,2,0,1:T(8,128)(2,1)S(1)}, u32[]{:S(2)}, u32[]{:S(2)}) %all-to-all-start) | async-done | bytes 1572896 | tf_op jit(solution)/shard_map/all_to_all | solution.py:91
  60.6 1.0 convolution_bitcast_fusion.2
  62.1 1.9 copy.79
  64.0 25.0 %all_to_all.84 = bf16[2,1,2,256,768]{4,0,2,1,3:T(2,128)(2,1)S(1)} all-to-all(bf16[2,1,2,256,768]{4,0,2,1,3:T(2,128)(2,1)S(1)} %copy.79), channel_id=1, replica_groups=mesh['lat'=8,'lon'=32] {'lat'}, dimensions={3} | all-to-all | bytes 3145728 | tf_op jit(solution)/shard_map/all_to_all | solution.py:121
  89.2 2.1 copy.81
  91.3 5.9 %all-to-all-start.2 = ((bf16[2,8,2,32,768]{4,1,2,0,3:T(8,128)(2,1)}), bf16[2,8,2,32,768]{4,1,2,0,3:T(8,128)(2,1)S(1)}, u32[]{:S(2)}, u32[]{:S(2)}) async-start(bf16[2,8,2,32,768]{4,1,2,0,3:T(8,128)(2,1)} %copy.81), calls=%async_computation.2 | async-start | bytes 3145728 | tf_op jit(solution)/shard_map/all_to_all | solution.py:120
  97.2 1.1 multiply_convert_fusion.9
  98.4 1.1 multiply_convert_fusion.12
  99.5 36.3 %all-to-all-done.2 = bf16[2,8,2,32,768]{4,1,2,0,3:T(8,128)(2,1)S(1)} async-done(((bf16[2,8,2,32,768]{4,1,2,0,3:T(8,128)(2,1)}), bf16[2,8,2,32,768]{4,1,2,0,3:T(8,128)(2,1)S(1)}, u32[]{:S(2)}, u32[]{:S(2)}) %all-to-all-start.2) | async-done | bytes 1572896 | tf_op jit(solution)/shard_map/all_to_all | solution.py:120
  135.8 1.0 convolution_bitcast_fusion.1
  136.8 0.4 fusion.4
  137.3 0.6 copy-done.2
  137.8 0.3 fusion.88
  138.1 0.3 fusion.96
  138.5 0.5 multiply_convert_fusion.4
  139.0 0.5 copy-done.7
  139.4 0.3 fusion.84
  139.8 0.3 fusion.76
  140.2 0.5 multiply_convert_fusion.3
  140.7 0.4 subtract_convert_fusion.1
  141.1 0.3 fusion.79
  141.4 0.4 subtract_convert_fusion
  141.8 0.2 fusion.81
  142.1 0.6 fusion.27
  142.7 0.2 fusion.91
  143.0 0.6 fusion.28
  143.6 0.2 fusion.93
  143.8 0.3 fusion.29
  144.1 0.3 fusion.30
  144.4 1.0 convolution_bitcast_fusion
  145.4 0.2 fusion.41
  145.9 3.1 copy.98
  149.1 25.3 %all_to_all.85 = bf16[2,256,2,1,768]{4,0,3,2,1:T(2,128)(2,1)S(1)} all-to-all(bf16[2,256,2,1,768]{4,0,3,2,1:T(2,128)(2,1)} %copy.98), channel_id=1, replica_groups=mesh['lat'=8,'lon'=32] {'lat'}, dimensions={1} | all-to-all | bytes 3145728 | tf_op jit(solution)/shard_map/all_to_all | solution.py:175
  174.6 2.1 copy.100
  176.6 6.0 %all-to-all-start.4 = ((bf16[2,32,2,8,768]{4,3,2,0,1:T(8,128)(2,1)}), bf16[2,32,2,8,768]{4,3,2,0,1:T(8,128)(2,1)S(1)}, u32[]{:S(2)}, u32[]{:S(2)}) async-start(bf16[2,32,2,8,768]{4,3,2,0,1:T(8,128)(2,1)} %copy.100), calls=%async_computation.4 | async-start | bytes 3145728 | tf_op jit(solution)/shard_map/all_to_all | solution.py:174
  182.7 3.2 multiply_convert_fusion.6
  185.9 1.2 fusion.127
  187.2 1.0 fusion.32
  188.2 0.3 fusion.128
  188.4 1.0 fusion.31
  189.5 1.0 fusion.125
  190.5 30.7 %all-to-all-done.4 = bf16[2,32,2,8,768]{4,3,2,0,1:T(8,128)(2,1)S(1)} async-done(((bf16[2,32,2,8,768]{4,3,2,0,1:T(8,128)(2,1)}), bf16[2,32,2,8,768]{4,3,2,0,1:T(8,128)(2,1)S(1)}, u32[]{:S(2)}, u32[]{:S(2)}) %all-to-all-start.4) | async-done | bytes 1572896 | tf_op jit(solution)/shard_map/all_to_all | solution.py:174
  221.4 0.8 copy-done.13
  222.3 0.6 fusion.18
  222.9 0.7 fusion.17
  223.7 3.0 copy.102
  226.7 5.9 %all-to-all-start.5 = ((bf16[2,1,512,768]{3,0,1,2:T(2,128)(2,1)}), bf16[2,1,512,768]{3,0,1,2:T(2,128)(2,1)S(1)}, u32[]{:S(2)}, u32[]{:S(2)}) async-start(bf16[2,1,512,768]{3,0,1,2:T(2,128)(2,1)} %copy.102), calls=%async_computation.5 | async-start | bytes 3145728 | tf_op jit(solution)/shard_map/all_to_all | solution.py:91
  232.7 2.0 pad_maximum_fusion.5
  234.7 0.3 fusion.34
  235.0 0.2 fusion.126
  235.2 0.3 fusion.33
  235.5 0.9 pad_maximum_fusion.4
  236.5 67.8 %all-reduce.7.cloned.1.call-done = (f32[2,8,96,96]{3,2,1,0:T(8,128)}, f32[2,8,96,96]{3,2,1,0:T(8,128)}) async-done(((f32[2,8,96,96]{3,2,1,0:T(8,128)}, f32[2,8,96,96]{3,2,1,0:T(8,128)}), (f32[2,8,96,96]{3,2,1,0:T(8,128)}, f32[2,8,96,96]{3,2,1,0:T(8,128)})) %all-reduce.7.cloned.1.call-update) | async-done | bytes 1179664 | tf_op jit(solution)/shard_map/psum | solution.py:205
  304.3 156.9 %all-reduce.5.cloned.1.call-done = (f32[2,8,96,96]{3,2,1,0:T(8,128)}, f32[2,8,96,96]{3,2,1,0:T(8,128)}) async-done(((f32[2,8,96,96]{3,2,1,0:T(8,128)}, f32[2,8,96,96]{3,2,1,0:T(8,128)}), (f32[2,8,96,96]{3,2,1,0:T(8,128)}, f32[2,8,96,96]{3,2,1,0:T(8,128)})) %all-reduce.5.cloned.1.call-update) | async-done | bytes 1179664 | tf_op jit(solution)/shard_map/psum | solution.py:205
  461.3 2.2 broadcast_multiply_fusion
  463.4 0.9 broadcast_multiply_fusion.1
  464.4 2.2 fusion.123
  466.7 1.0 copy-done.8
  467.7 1.1 fusion.13
  468.9 1.0 copy-done.9
  469.9 1.1 fusion.14
  (50 shorter events, 2.3 us)
Async XLA Ops:
  9.9 50.6 %all-to-all-start = ((bf16[2,32,16,768]{3,2,0,1:T(8,128)(2,1)}), bf16[2,32,16,768]{3,2,0,1:T(8,128)(2,1)S(1)}, u32[]{:S(2)}, u32[]{:S(2)}) async-start(bf16[2,32,16,768]{3,2,0,1:T(8,128)(2,1)} %pad_maximum_fusion), calls=%async_computation | async-start | bytes 3145728 | tf_op jit(solution)/shard_map/all_to_all | solution.py:91
  91.3 44.5 %all-to-all-start.2 = ((bf16[2,8,2,32,768]{4,1,2,0,3:T(8,128)(2,1)}), bf16[2,8,2,32,768]{4,1,2,0,3:T(8,128)(2,1)S(1)}, u32[]{:S(2)}, u32[]{:S(2)}) async-start(bf16[2,8,2,32,768]{4,1,2,0,3:T(8,128)(2,1)} %copy.81), calls=%async_computation.2 | async-start | bytes 3145728 | tf_op jit(solution)/shard_map/all_to_all | solution.py:120
  136.8 1.0 copy-start.2
  138.4 1.0 copy-start.7
  141.1 1.8 copy-start.3
  141.8 0.9 copy-start.5
  143.6 0.8 copy-start
  176.6 44.5 %all-to-all-start.4 = ((bf16[2,32,2,8,768]{4,3,2,0,1:T(8,128)(2,1)}), bf16[2,32,2,8,768]{4,3,2,0,1:T(8,128)(2,1)S(1)}, u32[]{:S(2)}, u32[]{:S(2)}) async-start(bf16[2,32,2,8,768]{4,3,2,0,1:T(8,128)(2,1)} %copy.100), calls=%async_computation.4 | async-start | bytes 3145728 | tf_op jit(solution)/shard_map/all_to_all | solution.py:174
  182.6 4.5 copy-start.6
  187.1 1.3 copy-start.4
  221.3 1.0 copy-start.13
  221.3 1.0 copy-start.14
  226.7 6.0 %copy-start.10 = (f32[1,8,96,96]{3,2,1,0:T(8,128)S(1)}, f32[1,8,96,96]{3,2,1,0:T(8,128)}, u32[]{:S(2)}) copy-start(f32[1,8,96,96]{3,2,1,0:T(8,128)} %fusion.32) | copy-start | bytes 884740
  226.7 237.7 %all-to-all-start.5 = ((bf16[2,1,512,768]{3,0,1,2:T(2,128)(2,1)}), bf16[2,1,512,768]{3,0,1,2:T(2,128)(2,1)S(1)}, u32[]{:S(2)}, u32[]{:S(2)}) async-start(bf16[2,1,512,768]{3,0,1,2:T(2,128)(2,1)} %copy.102), calls=%async_computation.5 | async-start | bytes 3145728 | tf_op jit(solution)/shard_map/all_to_all | solution.py:91
  232.6 2.1 copy-start.1
  232.6 71.7 %all-reduce.7.cloned.1.call-start = ((), (), s32[]{:S(2)}) async-start(), calls=%async_computation.7 | async-start | bytes 3145728 | tf_op jit(solution)/shard_map/psum | solution.py:205
  232.7 2.0 copy-start.11
  236.5 224.8 %all-reduce.5.cloned.1.call-start = ((), (), s32[]{:S(2)}) async-start(), calls=%async_computation.6 | async-start | bytes 3145728 | tf_op jit(solution)/shard_map/psum | solution.py:205
  461.3 2.2 copy-start.12
  466.6 1.1 copy-start.8
  468.8 1.1 copy-start.9
Sparse Core Ops, SparseCore 0:
  236.6 67.6 all-reduce.6
  307.8 153.4 all-reduce.4
